TPU v7x, 32 devices: a whole 2x2x4 slice. The times are simulated.
32 devices in a mesh: dp: 8 (over y, x, core), tensor: 4 (over z).
Axes of the slice: x: 2, y: 2, z: 4, core: 2. Of those that a mesh axis runs over, the one named last changes fastest.
Arguments:
- tokens: bfloat16 [4096, 768], P('dp'), may hold values from -6 to 6
- lengths: int32 [8, 16], P('dp'), may hold values from 0 to 512, as said below
- w_query: bfloat16 [768, 768], P(None, 'tensor'), may hold values from -0.21875 to 0.21875
- w_key: bfloat16 [768, 768], P(None, 'tensor'), may hold values from -0.21875 to 0.21875
- w_value: bfloat16 [768, 768], P(None, 'tensor'), may hold values from -0.21875 to 0.21875
- b_query: float32 [768], P('tensor'), may hold values from -3 to 3
- b_value: float32 [768], P('tensor'), may hold values from -3 to 3
- w_out: bfloat16 [768, 768], P('tensor'), may hold values from -0.625 to 0.625
- b_out: float32 [768], replicated, may hold values from -3 to 3
- g_attn: float32 [768], replicated, may hold values from 0.5 to 1.5
- b_attn: float32 [768], replicated, may hold values from -3 to 3
- w_up: bfloat16 [768, 3072], P(None, 'tensor'), may hold values from -0.21875 to 0.21875
- b_up: float32 [3072], P('tensor'), may hold values from -3 to 3
- w_down: bfloat16 [3072, 768], P('tensor'), may hold values from -0.109375 to 0.109375
- b_down: float32 [768], replicated, may hold values from -3 to 3
- g_ffn: float32 [768], replicated, may hold values from 0.5 to 1.5
- b_ffn: float32 [768], replicated, may hold values from -3 to 3
- out_grad: bfloat16 [4096, 768], P('dp'), may hold values from -6 to 6
- pool_grad: float32 [128, 1728], P('dp'), may hold values from -6 to 6
Outputs:
- layer_out: bfloat16 [4096, 768], P('dp')
- pools: float32 [128, 1728], replicated
- d_tokens: float32 [4096, 768], P('dp')
- d_w_query: float32 [768, 768], P(None, 'tensor')
- d_w_key: float32 [768, 768], P(None, 'tensor')
- d_w_value: float32 [768, 768], P(None, 'tensor')
- d_b_query: float32 [768], P('tensor')
- d_b_value: float32 [768], P('tensor')
- d_w_out: float32 [768, 768], P('tensor')
- d_b_out: float32 [768], replicated
- d_g_attn: float32 [768], replicated
- d_b_attn: float32 [768], replicated
- d_w_up: float32 [768, 3072], P(None, 'tensor')
- d_b_up: float32 [3072], P('tensor')
- d_w_down: float32 [3072, 768], P('tensor')
- d_b_down: float32 [768], replicated
- d_g_ffn: float32 [768], replicated
- d_b_ffn: float32 [768], replicated
Inputs may be any that keep to these rules, and one draw needn't show every extreme that they name: In each bucket the nonzero lengths come first and add up to at most 512; the first is nonzero; in every draw some bucket holds one sentence of exactly 512 tokens.
All inputs are finite; a program needn't handle non-finite values.
Results may differ from a plain program's by a relative error of at most 0.013.
Values sent between devices are 32-bit elements; how exact they have to be, the bound alone decides.
No kernel may reach another device: no remote copies, remote signals or barrier semaphores. Data moves between devices by JAX's collectives and lax.ppermute only.
A program may use at most 128 MiB of HBM per device.

v0:
```python
import jax
import jax.numpy as jnp
from jax import lax
from jax.sharding import PartitionSpec as P

HDIM = 64
SENTS = 16
norm_eps = 1e-06
pool_eps = 1e-05
highest = lax.Precision.HIGHEST


def truncations(width):
    return [width, width * 2 // 3, width // 3, width // 6, width // 12]


def segment_ids(sizes, slot_count):
    ends = jnp.cumsum(sizes, dtype=jnp.int32)
    places = jnp.arange(slot_count, dtype=jnp.int32)
    return jnp.sum((places[:, None] >= ends[None, :]).astype(jnp.int32), axis=1)


def norm_stats(rows):
    centre = jnp.mean(rows, axis=-1, keepdims=True)
    shifted = rows - centre
    inverse = lax.rsqrt(jnp.mean(shifted * shifted, axis=-1, keepdims=True) + norm_eps)
    return (shifted * inverse, inverse)


def norm_back(grad_in, normal, inverse):
    centre = jnp.mean(grad_in, axis=-1, keepdims=True)
    along = jnp.mean(grad_in * normal, axis=-1, keepdims=True)
    return inverse * (grad_in - centre - normal * along)


def gelu_exact(upper):
    return jax.nn.gelu(upper, approximate=False)


def attention_scores(query_heads, key_heads, allowed, score_scale):
    scores = (
        jnp.einsum("qhd,khd->hqk", query_heads, key_heads, preferred_element_type=jnp.float32)
        * score_scale
    )
    return jnp.where(allowed[None], scores, -1000000000.0)


def shards(
    tokens,
    lengths,
    w_query,
    w_key,
    w_value,
    b_query,
    b_value,
    w_out,
    b_out,
    g_attn,
    b_attn,
    w_up,
    b_up,
    w_down,
    b_down,
    g_ffn,
    b_ffn,
    out_grad,
    pool_grad,
):
    slot_count = tokens.shape[0]
    model_width = tokens.shape[1]
    local_cols = w_query.shape[1]
    head_count = local_cols // HDIM
    score_scale = HDIM ** (-0.5)
    segment = segment_ids(lengths[0], slot_count)
    allowed = segment[:, None] == segment[None, :]
    inputs = tokens.astype(jnp.float32)
    query_rows = (jnp.dot(tokens, w_query, preferred_element_type=jnp.float32) + b_query).astype(
        jnp.bfloat16
    )
    key_rows = jnp.dot(tokens, w_key, preferred_element_type=jnp.float32).astype(jnp.bfloat16)
    value_rows = (jnp.dot(tokens, w_value, preferred_element_type=jnp.float32) + b_value).astype(
        jnp.bfloat16
    )
    query_heads = query_rows.reshape(slot_count, head_count, HDIM)
    key_heads = key_rows.reshape(slot_count, head_count, HDIM)
    value_heads = value_rows.reshape(slot_count, head_count, HDIM)
    scores = attention_scores(query_heads, key_heads, allowed, score_scale)
    top_score = jnp.max(scores, axis=-1, keepdims=True)
    log_total = top_score + jnp.log(jnp.sum(jnp.exp(scores - top_score), axis=-1, keepdims=True))
    probs_low = jnp.exp(scores - log_total).astype(jnp.bfloat16)
    mixed = jnp.einsum("hqk,khd->qhd", probs_low, value_heads, preferred_element_type=jnp.float32)
    mixed = mixed.reshape(slot_count, local_cols).astype(jnp.bfloat16)
    partial_value = jnp.dot(mixed, w_out, preferred_element_type=jnp.float32)
    attn_total = lax.psum(partial_value, "tensor")
    normal_attn, inverse_attn = norm_stats(inputs + attn_total + b_out)
    normed = normal_attn * g_attn + b_attn
    normed_low = normed.astype(jnp.bfloat16)
    upper = jnp.dot(normed_low, w_up, preferred_element_type=jnp.float32) + b_up
    act_rows = gelu_exact(upper).astype(jnp.bfloat16)
    down_total = lax.psum(jnp.dot(act_rows, w_down, preferred_element_type=jnp.float32), "tensor")
    normal_ffn, inverse_ffn = norm_stats(normed + down_total + b_down)
    final = normal_ffn * g_ffn + b_ffn
    layer_out = final.astype(jnp.bfloat16)
    sentence = jnp.arange(SENTS, dtype=jnp.int32)
    member = (segment[None, :] == sentence[:, None]).astype(jnp.float32)
    denom = jnp.maximum(lengths[0], 1).astype(jnp.float32)[:, None]
    pooled = jnp.dot(member, final, precision=highest, preferred_element_type=jnp.float32) / denom
    pieces = []
    factors = []
    for keep_width in truncations(model_width):
        leading = pooled[:, :keep_width]
        factor = lax.rsqrt(jnp.mean(leading * leading, axis=1, keepdims=True) + pool_eps)
        pieces.append(leading * factor)
        factors.append(factor)
    pools = lax.all_gather(jnp.concatenate(pieces, axis=1), "dp", axis=0, tiled=True)
    d_pooled = jnp.zeros_like(pooled)
    offset = 0
    for keep_width, factor in zip(truncations(model_width), factors):
        leading = pooled[:, :keep_width]
        upstream = pool_grad[:, offset : offset + keep_width]
        inner = jnp.mean(upstream * leading, axis=1, keepdims=True)
        d_pooled = d_pooled.at[:, :keep_width].add(factor * upstream - leading * factor**3 * inner)
        offset = offset + keep_width
    spread_back = jnp.einsum(
        "st,sd->td", member, d_pooled / denom, precision=highest, preferred_element_type=jnp.float32
    )
    d_final = out_grad.astype(jnp.float32) + spread_back
    g_ffn_part = jnp.sum(d_final * normal_ffn, axis=0)
    b_ffn_part = jnp.sum(d_final, axis=0)
    d_resid = norm_back(d_final * g_ffn, normal_ffn, inverse_ffn)
    b_down_part = jnp.sum(d_resid, axis=0)
    resid_low = d_resid.astype(jnp.bfloat16)
    w_down_part = jnp.einsum("tf,td->fd", act_rows, resid_low, preferred_element_type=jnp.float32)
    d_act = jnp.einsum("td,fd->tf", resid_low, w_down, preferred_element_type=jnp.float32)
    d_upper = jax.vjp(gelu_exact, upper)[1](d_act)[0]
    b_up_part = jnp.sum(d_upper, axis=0)
    upper_low = d_upper.astype(jnp.bfloat16)
    w_up_part = jnp.einsum("td,tf->df", normed_low, upper_low, preferred_element_type=jnp.float32)
    normed_term = jnp.einsum("tf,df->td", upper_low, w_up, preferred_element_type=jnp.float32)
    d_normed = d_resid + lax.psum(normed_term, "tensor")
    g_attn_part = jnp.sum(d_normed * normal_attn, axis=0)
    b_attn_part = jnp.sum(d_normed, axis=0)
    d_hidden = norm_back(d_normed * g_attn, normal_attn, inverse_attn)
    b_out_part = jnp.sum(d_hidden, axis=0)
    hidden_low = d_hidden.astype(jnp.bfloat16)
    w_out_part = jnp.einsum("tc,td->cd", mixed, hidden_low, preferred_element_type=jnp.float32)
    d_mixed = jnp.einsum("td,cd->tc", hidden_low, w_out, preferred_element_type=jnp.float32)
    d_mixed = d_mixed.astype(jnp.bfloat16).reshape(slot_count, head_count, HDIM)
    scores_again = attention_scores(query_heads, key_heads, allowed, score_scale)
    probs = jnp.exp(scores_again - log_total)
    probs_again = probs.astype(jnp.bfloat16)
    d_probs = jnp.einsum("qhd,khd->hqk", d_mixed, value_heads, preferred_element_type=jnp.float32)
    row_inner = jnp.sum(probs * d_probs, axis=-1, keepdims=True)
    d_scores = (probs * (d_probs - row_inner) * score_scale).astype(jnp.bfloat16)
    d_query = jnp.einsum(
        "hqk,khd->qhd", d_scores, key_heads, preferred_element_type=jnp.float32
    ).reshape(slot_count, local_cols)
    d_key = jnp.einsum(
        "hqk,qhd->khd", d_scores, query_heads, preferred_element_type=jnp.float32
    ).reshape(slot_count, local_cols)
    d_value = jnp.einsum(
        "hqk,qhd->khd", probs_again, d_mixed, preferred_element_type=jnp.float32
    ).reshape(slot_count, local_cols)
    b_query_part = jnp.sum(d_query, axis=0)
    b_value_part = jnp.sum(d_value, axis=0)
    query_low = d_query.astype(jnp.bfloat16)
    key_low = d_key.astype(jnp.bfloat16)
    value_low = d_value.astype(jnp.bfloat16)
    w_query_part = jnp.einsum("td,tc->dc", tokens, query_low, preferred_element_type=jnp.float32)
    w_key_part = jnp.einsum("td,tc->dc", tokens, key_low, preferred_element_type=jnp.float32)
    w_value_part = jnp.einsum("td,tc->dc", tokens, value_low, preferred_element_type=jnp.float32)
    input_term = jnp.einsum("tc,dc->td", query_low, w_query, preferred_element_type=jnp.float32)
    input_term = input_term + jnp.einsum(
        "tc,dc->td", key_low, w_key, preferred_element_type=jnp.float32
    )
    input_term = input_term + jnp.einsum(
        "tc,dc->td", value_low, w_value, preferred_element_type=jnp.float32
    )
    d_tokens = d_hidden + lax.psum(input_term, "tensor")
    grad_sums = lax.psum(
        (
            w_query_part,
            w_key_part,
            w_value_part,
            b_query_part,
            b_value_part,
            w_out_part,
            b_out_part,
            g_attn_part,
            b_attn_part,
            w_up_part,
            b_up_part,
            w_down_part,
            b_down_part,
            g_ffn_part,
            b_ffn_part,
        ),
        "dp",
    )
    (
        d_w_query,
        d_w_key,
        d_w_value,
        d_b_query,
        d_b_value,
        d_w_out,
        d_b_out,
        d_g_attn,
        d_b_attn,
        d_w_up,
        d_b_up,
        d_w_down,
        d_b_down,
        d_g_ffn,
        d_b_ffn,
    ) = grad_sums
    return (
        layer_out,
        pools,
        d_tokens,
        d_w_query,
        d_w_key,
        d_w_value,
        d_b_query,
        d_b_value,
        d_w_out,
        d_b_out,
        d_g_attn,
        d_b_attn,
        d_w_up,
        d_b_up,
        d_w_down,
        d_b_down,
        d_g_ffn,
        d_b_ffn,
    )


def solution(mesh):
    return jax.shard_map(
        shards,
        mesh=mesh,
        in_specs=(
            P("dp", None),
            P("dp", None),
            P(None, "tensor"),
            P(None, "tensor"),
            P(None, "tensor"),
            P("tensor"),
            P("tensor"),
            P("tensor", None),
            P(),
            P(),
            P(),
            P(None, "tensor"),
            P("tensor"),
            P("tensor", None),
            P(),
            P(),
            P(),
            P("dp", None),
            P("dp", None),
        ),
        out_specs=(
            P("dp", None),
            P(),
            P("dp", None),
            P(None, "tensor"),
            P(None, "tensor"),
            P(None, "tensor"),
            P("tensor"),
            P("tensor"),
            P("tensor", None),
            P(),
            P(),
            P(),
            P(None, "tensor"),
            P("tensor"),
            P("tensor", None),
            P(),
            P(),
            P(),
        ),
        check_vma=False,
    )
```

profile of v0, /device:TPU:0, one launch (start us, length us, event | category | flops | bytes accessed | tf_op | source)
XLA Modules:
  0.0 486.1 jit_solution(11460330406638272772)
XLA Ops:
  7.3 0.9 copy.49
  8.6 1.7 convolution_convert_fusion.2
  13.3 1.0 convolution_convert_fusion
  14.3 1.6 fusion.70
  16.0 71.8 %all-reduce.8.cloned.1.call-done = f32[512,768]{1,0:T(8,128)} async-done(((f32[512,768]{1,0:T(8,128)}), f32[512,768]{1,0:T(8,128)}) %all-reduce.8.cloned.1.call-update) | async-done | bytes 1572880 | tf_op jit(solution)/shard_map/psum | solution.py:94
  87.7 1.7 fusion.64
  90.2 5.4 %multiply_convert_fusion.1 = (bf16[512,768]{1,0:T(8,128)(2,1)S(1)}, f32[512,768]{1,0:T(8,128)}, f32[512,768]{1,0:T(8,128)}) fusion(f32[768]{0:T(1024)S(1)} %copy-done.59, bf16[768,768]{1,0:T(8,128)(2,1)S(1)} %copy-done, f32[512,768]{1,0:T(8,128)S(1)} %get-tuple-element.189, f32[768]{0:T(1024)S(1)} %copy-done.53, f32[768]{0:T(1024)S(1)} %copy-done.35, ...), kind=kOutput, calls=%fused_computation.24 | convolution fusion | flops 631898112 | bytes 6697984 | tf_op jit(solution)/shard_map/dot_general | solution.py:98
  95.5 0.9 copy-done.16
  96.4 1.9 fusion.71
  99.9 1.2 convert_bitcast_fusion
  101.0 65.6 %all-reduce.10.cloned.1.call-done = f32[512,768]{1,0:T(8,128)} async-done(((f32[512,768]{1,0:T(8,128)}), f32[512,768]{1,0:T(8,128)}) %all-reduce.10.cloned.1.call-update) | async-done | bytes 1572880 | tf_op jit(solution)/shard_map/psum | solution.py:100
  166.7 2.0 fusion.62
  169.7 1.0 multiply_reduce_fusion.9
  173.5 1.3 add_select_fusion.2
  175.5 1.4 scatter-add.19
  177.0 3.9 multiply_reduce_fusion.1
  181.0 1.5 fusion.60
  183.5 1.8 fusion.69
  185.3 0.9 copy-done.63
  186.2 2.0 fusion.42
  188.4 68.0 %all-reduce.12.cloned.1.call-done = f32[512,768]{1,0:T(8,128)} async-done(((f32[512,768]{1,0:T(8,128)}), f32[512,768]{1,0:T(8,128)}) %all-reduce.12.cloned.1.call-update) | async-done | bytes 1572880 | tf_op jit(solution)/shard_map/psum | solution.py:140
  256.4 3.3 multiply_reduce_fusion.2
  259.8 1.1 fusion.61
  260.9 1.1 copy-done.2
  262.5 2.3 fusion.72
  264.8 7.5 %fusion.66 = (f32[3,64]{1,0:T(4,128)}, bf16[512,3,64]{0,2,1:T(8,128)(2,1)S(1)}) fusion(bf16[512,3,64]{0,2,1:T(8,128)(2,1)S(1)} %bitcast.68, f32[3,512,512]{1,2,0:T(8,128)} %fusion.72, f32[3,512]{1,0:T(4,128)S(1)} %copy-done.44, f32[3,512,512]{1,2,0:T(8,128)} %copy-done.8, pred[512,512]{0,1:T(8,128)(4,1)S(1)} %copy-done.12), kind=kOutput, calls=%fused_computation.151 | convolution fusion | flops 109512512 | bytes 6953728 | tf_op jit(solution)/shard_map/hqk,khd->qhd/dot_general | solution.py:155
  272.3 6.9 %fusion.27 = bf16[3,64,512]{2,1,0:T(8,128)(2,1)S(1)} fusion(bf16[512,3,64]{0,2,1:T(8,128)(2,1)} %bitcast.78, f32[3,512,512]{1,2,0:T(8,128)} %fusion.72, f32[3,512,512]{1,2,0:T(8,128)} %copy-done.8, f32[3,512]{1,0:T(4,128)S(1)} %copy-done.44, pred[512,512]{0,1:T(8,128)(4,1)S(1)} %copy-done.12), kind=kOutput, calls=%fused_computation.60 | convolution fusion | flops 109414400 | bytes 6952960 | tf_op jit(solution)/shard_map/hqk,qhd->khd/dot_general | solution.py:158
  279.3 3.6 fusion.65
  284.2 1.6 add_add_fusion
  285.9 3.9 fusion.44
  289.8 2.4 fusion.40
  292.2 1.1 convolution_bitcast_fusion.2
  293.4 1.1 convolution_bitcast_fusion.1
  294.5 1.1 convolution_bitcast_fusion
  295.7 1.1 fusion.37
  297.7 10.6 %all_gather.3 = f32[128,1728]{1,0:T(8,128)S(1)} all-gather(f32[16,1728]{1,0:T(8,128)S(1)} %copy-done.30), channel_id=1, replica_groups=mesh['dp'=8,'tensor'=4] {'dp'}, dimensions={0}, use_global_device_ids=true | all-gather | bytes 995328 | tf_op jit(solution)/shard_map/all_gather | solution.py:115
  308.3 1.2 copy.54
  309.7 25.0 %all-reduce = (f32[192]{0:T(256)}, f32[192]{0:T(256)}, f32[768]{0:T(1024)}, f32[768]{0:T(1024)}, f32[768]{0:T(1024)}, /*index=5*/f32[768]{0:T(1024)}, f32[768]{0:T(1024)}, f32[768]{0:T(1024)}, f32[768]{0:T(1024)}) all-reduce(f32[192]{0:T(256)S(1)} %reduce_sum.296, ...), channel_id=1, replica_groups=mesh['dp'=8,'tensor'=4] {'dp'}, use_global_device_ids=true, to_apply=%region_35.36 | all-reduce | flops 5760 | bytes 46080 | tf_op jit(solution)/shard_map/psum | solution.py:180
  334.7 19.3 %all-reduce.14.cloned.1.call-done = f32[512,768]{1,0:T(8,128)} async-done(((f32[512,768]{1,0:T(8,128)}), f32[512,768]{1,0:T(8,128)}) %all-reduce.14.cloned.1.call-update) | async-done | bytes 1572880 | tf_op jit(solution)/shard_map/psum | solution.py:179
  354.1 2.7 add.261
  356.8 114.3 %all-reduce.16.cloned.1.call-done = (f32[768,192]{0,1:T(8,128)}, f32[768,192]{0,1:T(8,128)}, f32[768,192]{0,1:T(8,128)}, f32[192,768]{1,0:T(8,128)}, f32[768,768]{1,0:T(8,128)}, /*index=5*/f32[768,768]{1,0:T(8,128)}) async-done(((f32[768,192]{0,1:T(8,128)}, f32[768,192]{0,1:T(8,128)}, f32[768,192]{0,1:T(8,128)}, f32[192,768]{1,0:T(8,128)}, f32[768,768]{1,0:T(8,128)}, /*index=5*/f32[768,768]{1,0:T(8,128)}), ...) | async-done | bytes 7077904 | tf_op jit(solution)/shard_map/psum | solution.py:180
  471.1 2.0 copy.77
  473.2 0.8 copy.78
  474.0 0.8 copy.79
  474.8 0.8 copy.80
  475.6 1.4 copy.81
  477.0 1.1 copy-done.9
  478.1 1.4 copy.82
  (179 shorter events, 14.3 us)
Async XLA Ops:
  7.2 82.6 %copy-start = (bf16[768,768]{1,0:T(8,128)(2,1)S(1)}, bf16[768,768]{1,0:T(8,128)(2,1)}, u32[]{:S(2)}) copy-start(bf16[768,768]{1,0:T(8,128)(2,1)} %param.42) | copy-start | bytes 3538948
  7.2 3.1 copy-start.4
  7.2 3.1 copy-start.26
  7.2 3.1 copy-start.60
  7.2 80.5 %all-reduce.8.cloned.1.call-start = ((), (), s32[]{:S(2)}) async-start(), calls=%async_computation | async-start | bytes 3145728 | tf_op jit(solution)/shard_map/psum | solution.py:94
  8.6 4.6 copy-start.11
  11.6 1.7 copy-start.8
  14.3 73.4 %copy-start.52 = (f32[768]{0:T(1024)S(1)}, f32[768]{0:T(1024)}, u32[]{:S(2)}) copy-start(f32[768]{0:T(1024)} %param.39) | copy-start | bytes 9220
  15.9 150.8 %all-reduce.10.cloned.1.call-start = ((), (), s32[]{:S(2)}) async-start(), calls=%async_computation.1 | async-start | bytes 3145728 | tf_op jit(solution)/shard_map/psum | solution.py:100
  90.1 6.3 %copy-start.57 = (bf16[768,768]{1,0:T(8,128)(2,1)S(1)}, bf16[768,768]{1,0:T(8,128)(2,1)}, u32[]{:S(2)}) copy-start(bf16[768,768]{1,0:T(8,128)(2,1)} %param.44) | copy-start | bytes 3538948
  98.4 158.1 %all-reduce.12.cloned.1.call-start = ((), (), s32[]{:S(2)}) async-start(), calls=%async_computation.2 | async-start | bytes 3145728 | tf_op jit(solution)/shard_map/psum | solution.py:140
  168.6 2.1 copy-start.5
  168.7 2.0 copy-start.36
  169.7 5.9 %copy-start.41 = (f32[512]{0:T(512)}, f32[512]{0:T(512)S(1)}, u32[]{:S(2)}) copy-start(f32[512]{0:T(512)S(1)} %add_rsqrt_fusion) | copy-start | bytes 6148
  173.5 2.0 copy-start.34
  176.9 4.0 copy-start.6
  176.9 4.0 copy-start.37
  176.9 4.0 copy-start.42
  176.9 4.0 copy-start.46
  176.9 4.0 copy-start.48
  180.9 2.0 copy-start.65
  180.9 2.6 copy-start.66
  182.5 2.8 copy-start.7
  188.2 165.9 %all-reduce.14.cloned.1.call-start = ((), (), s32[]{:S(2)}) async-start(), calls=%async_computation.3 | async-start | bytes 3145728 | tf_op jit(solution)/shard_map/psum | solution.py:179
  259.8 2.2 copy-start.15
  262.4 2.4 copy-start.12
  262.5 2.3 copy-start.20
  262.5 2.3 copy-start.44
  279.3 3.6 copy-start.27
  285.8 4.0 copy-start.54
  285.8 185.3 %all-reduce.16.cloned.1.call-start = ((), (), s32[]{:S(2)}) async-start(), calls=%async_computation.4 | async-start | bytes 14155776 | tf_op jit(solution)/shard_map/psum | solution.py:180
  285.9 3.9 copy-start.64
  293.4 2.3 copy-start.3
  293.4 2.3 copy-start.18
  296.8 12.7 %copy-start.55 = (f32[3,64]{1,0:T(4,128)S(1)}, f32[3,64]{1,0:T(4,128)}, u32[]{:S(2)}) copy-start(f32[3,64]{1,0:T(4,128)} %get-tuple-element.193) | copy-start | bytes 2308
  296.8 12.8 %copy-start.56 = (f32[3,64]{1,0:T(4,128)S(1)}, f32[3,64]{1,0:T(4,128)}, u32[]{:S(2)}) copy-start(f32[3,64]{1,0:T(4,128)} %get-tuple-element.191) | copy-start | bytes 2308
  296.9 12.9 %copy-start.38 = (f32[768]{0:T(1024)S(1)}, f32[768]{0:T(1024)}, u32[]{:S(2)}) copy-start(f32[768]{0:T(1024)} %get-tuple-element.175) | copy-start | bytes 9220
  296.9 12.8 %copy-start.39 = (f32[768]{0:T(1024)S(1)}, f32[768]{0:T(1024)}, u32[]{:S(2)}) copy-start(f32[768]{0:T(1024)} %get-tuple-element.142) | copy-start | bytes 9220
  296.9 12.8 %copy-start.40 = (f32[768]{0:T(1024)S(1)}, f32[768]{0:T(1024)}, u32[]{:S(2)}) copy-start(f32[768]{0:T(1024)} %get-tuple-element.147) | copy-start | bytes 9220
  296.9 12.8 %copy-start.49 = (f32[768]{0:T(1024)S(1)}, f32[768]{0:T(1024)}, u32[]{:S(2)}) copy-start(f32[768]{0:T(1024)} %get-tuple-element.140) | copy-start | bytes 9220
  296.9 12.8 %copy-start.50 = (f32[768]{0:T(1024)S(1)}, f32[768]{0:T(1024)}, u32[]{:S(2)}) copy-start(f32[768]{0:T(1024)} %get-tuple-element.146) | copy-start | bytes 9220
  296.9 12.8 %copy-start.51 = (f32[768]{0:T(1024)S(1)}, f32[768]{0:T(1024)}, u32[]{:S(2)}) copy-start(f32[768]{0:T(1024)} %get-tuple-element.219) | copy-start | bytes 9220
  471.1 2.1 copy-start.23
  471.1 2.9 copy-start.22
  471.1 3.7 copy-start.21
  473.2 2.5 copy-start.10
  475.6 2.5 copy-start.9
  475.6 3.9 copy-start.1
  (24 other events, 25.5 us)
Sparse Core Ops, SparseCore 0:
  16.0 71.6 all-reduce.7
  98.5 68.1 all-reduce.9
  188.3 68.1 all-reduce.11
  285.9 68.0 all-reduce.13
  359.1 111.9 all-reduce.15
where the time goes:
time: 487 us; the launch traced here: 486 us
  waiting for transfers between devices  339 us (70%)
  matrix products  55.8 us (11%)
  blocking collectives  35.6 us (7%)
  other arithmetic  20.7 us (4%)
  local copies, waits for them, and re-layouts  19.7 us (4%)
  between operations  14.5 us (3%)
    psum x1, waiting for transfers between devices, shards(): lax.psum((w_query_part, w_key_part, w_value_part, b_query_part, b_value_p...  114 us
    psum x1, waiting for transfers between devices, shards(): attn_total = lax.psum(partial_value, 'tensor')  71.8 us
    psum x1, waiting for transfers between devices, shards(): d_normed = d_resid + lax.psum(normed_term, 'tensor')  68 us
    psum x1, waiting for transfers between devices, shards(): lax.psum(jnp.dot(act_rows, w_down, preferred_element_type=jnp.float32), '...  65.6 us
    psum x1, blocking collectives, shards(): lax.psum((w_query_part, w_key_part, w_value_part, b_query_part, b_value_p...  25 us
    psum x1, waiting for transfers between devices, shards(): d_tokens = d_hidden + lax.psum(input_term, 'tensor')  19.3 us
    unnamed x141, local copies, waits for them, and re-layouts  17.3 us
    all_gather x1, blocking collectives, shards(): lax.all_gather(jnp.concatenate(pieces, axis=1), 'dp', axis=0, tiled=True)  10.6 us
  transfers between devices with their start and end apart: 5, of which 5 were waited for; matrix products, arithmetic and copies ran while one was open for 4% of the time, Pallas kernels for 0%

commit v1 on v0

--- a/solution.py
+++ b/solution.py
@@ -8,6 +8,17 @@
 norm_eps = 1e-06
 pool_eps = 1e-05
 highest = lax.Precision.HIGHEST
+
+
+def _proceed_types(piece_in):
+    which_axis = "tensor"
+    wide_out = piece_in
+    axis_total = lax.axis_size(which_axis)
+    for jj in [
+        [(j0, j0 ^ w) for j0 in range(axis_total)] for w in (1, 2, 4, 8, 16) if w < axis_total
+    ]:
+        wide_out = wide_out + lax.ppermute(wide_out, which_axis, jj)
+    return wide_out
 
 
 def truncations(width):
@@ -91,7 +102,7 @@
     mixed = jnp.einsum("hqk,khd->qhd", probs_low, value_heads, preferred_element_type=jnp.float32)
     mixed = mixed.reshape(slot_count, local_cols).astype(jnp.bfloat16)
     partial_value = jnp.dot(mixed, w_out, preferred_element_type=jnp.float32)
-    attn_total = lax.psum(partial_value, "tensor")
+    attn_total = _proceed_types(partial_value)
     normal_attn, inverse_attn = norm_stats(inputs + attn_total + b_out)
     normed = normal_attn * g_attn + b_attn
     normed_low = normed.astype(jnp.bfloat16)

time: 487 us -> 518 us (1.064)
  waiting for transfers between devices: 339 us -> 371 us
  starting transfers between devices: 0.61 us -> 6.5 us
    ppermute x0 -> x2, waiting for transfers between devices: none -> 102 us  [_proceed_types(): wide_out = wide_out + lax.ppermute(wide_out, which_axis, jj)]
    psum x1 -> x0, waiting for transfers between devices: 71.8 us -> none  [shards(): attn_total = lax.psum(partial_value, 'tensor')]
    ppermute x0 -> x2, starting transfers between devices: none -> 5.94 us  [_proceed_types(): wide_out = wide_out + lax.ppermute(wide_out, which_axis, jj)]
    unnamed x141 -> x133, local copies, waits for them, and re-layouts: 17.3 us -> 17.7 us
  transfers between devices with their start and end apart: 5 -> 6, of which waited for: 5 -> 6; matrix products, arithmetic and copies ran while one was open for 4% -> 3% of each run, Pallas kernels for 0% -> 0%
where the time goes in v1:
time: 518 us
  waiting for transfers between devices  371 us (72%)
  matrix products  51.7 us (10%)
  blocking collectives  35.6 us (7%)
  local copies, waits for them, and re-layouts  20.1 us (4%)
  other arithmetic  18.4 us (4%)
  between operations  14.5 us (3%)
  starting transfers between devices  6.5 us (1%)
    psum x1, waiting for transfers between devices, shards(): lax.psum((w_query_part, w_key_part, w_value_part, b_query_part, b_value_p...  114 us
    ppermute x2, waiting for transfers between devices, _proceed_types(): wide_out = wide_out + lax.ppermute(wide_out, which_axis, jj)  102 us
    psum x1, waiting for transfers between devices, shards(): d_normed = d_resid + lax.psum(normed_term, 'tensor')  68 us
    psum x1, waiting for transfers between devices, shards(): lax.psum(jnp.dot(act_rows, w_down, preferred_element_type=jnp.float32), '...  67.5 us
    psum x1, blocking collectives, shards(): lax.psum((w_query_part, w_key_part, w_value_part, b_query_part, b_value_p...  25 us
    psum x1, waiting for transfers between devices, shards(): d_tokens = d_hidden + lax.psum(input_term, 'tensor')  19.4 us
    unnamed x133, local copies, waits for them, and re-layouts  17.7 us
    all_gather x1, blocking collectives, shards(): lax.all_gather(jnp.concatenate(pieces, axis=1), 'dp', axis=0, tiled=True)  10.6 us
  transfers between devices with their start and end apart: 6, of which 6 were waited for; matrix products, arithmetic and copies ran while one was open for 3% of the time, Pallas kernels for 0%

profile of v1, /device:TPU:0, one launch (start us, length us, event | category | flops | bytes accessed | tf_op | source)
XLA Modules:
  0.0 517.9 jit_solution(4581010289319718198)
XLA Ops:
  7.3 0.9 copy.49
  8.6 1.7 convolution_convert_fusion.2
  13.3 1.0 convolution_convert_fusion
  14.7 3.1 collective-permute-start
  17.8 34.4 %collective-permute-done = f32[512,768]{1,0:T(8,128)S(1)} collective-permute-done((f32[512,768]{1,0:T(8,128)S(1)}, f32[512,768]{1,0:T(8,128)S(1)}, u32[]{:S(2)}, u32[]{:S(2)}) %collective-permute-start) | collective-permute-done | bytes 1572896 | tf_op jit(solution)/shard_map/ppermute | solution.py:20
  52.4 2.8 collective-permute-start.1
  55.3 67.4 %collective-permute-done.1 = f32[512,768]{1,0:T(8,128)S(1)} collective-permute-done((f32[512,768]{1,0:T(8,128)S(1)}, f32[512,768]{1,0:T(8,128)S(1)}, u32[]{:S(2)}, u32[]{:S(2)}) %collective-permute-start.1) | collective-permute-done | bytes 1572896 | tf_op jit(solution)/shard_map/ppermute | solution.py:20
  123.8 5.4 %multiply_convert_fusion.1 = (bf16[512,768]{1,0:T(8,128)(2,1)S(1)}, f32[512,768]{1,0:T(8,128)}, f32[512,768]{1,0:T(8,128)}) fusion(f32[768]{0:T(1024)S(1)} %copy-done.55, bf16[768,768]{1,0:T(8,128)(2,1)S(1)} %copy-done, f32[512,768]{1,0:T(8,128)S(1)} %get-tuple-element.189, f32[768]{0:T(1024)S(1)} %copy-done.51, f32[768]{0:T(1024)S(1)} %copy-done.36, ...), kind=kOutput, calls=%fused_computation.24 | convolution fusion | flops 631898112 | bytes 6697984 | tf_op jit(solution)/shard_map/dot_general | solution.py:109
  129.1 0.9 copy-done.17
  130.0 1.9 fusion.71
  133.5 1.2 convert_bitcast_fusion
  134.7 67.5 %all-reduce.7.cloned.1.call-done = f32[512,768]{1,0:T(8,128)} async-done(((f32[512,768]{1,0:T(8,128)}), f32[512,768]{1,0:T(8,128)}) %all-reduce.7.cloned.1.call-update) | async-done | bytes 1572880 | tf_op jit(solution)/shard_map/psum | solution.py:111
  202.1 2.0 fusion.62
  205.2 1.0 multiply_reduce_fusion.9
  209.0 1.3 add_select_fusion.2
  211.0 1.4 scatter-add.19
  212.4 3.9 multiply_reduce_fusion.1
  216.4 1.5 fusion.60
  219.0 1.8 fusion.69
  220.8 0.9 copy-done.59
  221.6 2.0 fusion.42
  223.9 68.0 %all-reduce.9.cloned.1.call-done = f32[512,768]{1,0:T(8,128)} async-done(((f32[512,768]{1,0:T(8,128)}), f32[512,768]{1,0:T(8,128)}) %all-reduce.9.cloned.1.call-update) | async-done | bytes 1572880 | tf_op jit(solution)/shard_map/psum | solution.py:151
  291.9 2.7 multiply_reduce_fusion.2
  296.1 1.2 copy-done.9
  297.3 1.1 fusion.65
  298.3 2.3 fusion.72
  300.7 7.0 %fusion.66 = (f32[3,64]{1,0:T(4,128)S(1)}, bf16[512,3,64]{0,2,1:T(8,128)(2,1)S(1)}) fusion(bf16[512,3,64]{0,2,1:T(8,128)(2,1)S(1)} %bitcast.68, f32[3,512,512]{1,2,0:T(8,128)} %fusion.72, f32[3,512]{1,0:T(4,128)S(1)} %copy-done.42, f32[3,512,512]{1,2,0:T(8,128)} %copy-done.8, pred[512,512]{0,1:T(8,128)(4,1)S(1)} %copy-done.13), kind=kOutput, calls=%fused_computation.151 | convolution fusion | flops 109512512 | bytes 6953728 | tf_op jit(solution)/shard_map/hqk,khd->qhd/dot_general | solution.py:166
  307.6 6.9 %fusion.27 = bf16[3,64,512]{2,1,0:T(8,128)(2,1)S(1)} fusion(bf16[512,3,64]{0,2,1:T(8,128)(2,1)} %bitcast.78, f32[3,512,512]{1,2,0:T(8,128)} %fusion.72, f32[3,512,512]{1,2,0:T(8,128)} %copy-done.8, f32[3,512]{1,0:T(4,128)S(1)} %copy-done.42, pred[512,512]{0,1:T(8,128)(4,1)S(1)} %copy-done.13), kind=kOutput, calls=%fused_computation.60 | convolution fusion | flops 109414400 | bytes 6952960 | tf_op jit(solution)/shard_map/hqk,qhd->khd/dot_general | solution.py:169
  316.0 1.6 add_add_fusion
  317.6 3.9 fusion.44
  321.6 2.4 fusion.40
  324.0 1.1 convolution_bitcast_fusion
  325.1 1.1 convolution_bitcast_fusion.1
  326.3 1.1 convolution_bitcast_fusion.2
  327.4 1.1 fusion.37
  328.6 0.8 copy-done.31
  329.5 10.6 %all_gather.3 = f32[128,1728]{1,0:T(8,128)S(1)} all-gather(f32[16,1728]{1,0:T(8,128)S(1)} %copy-done.31), channel_id=1, replica_groups=mesh['dp'=8,'tensor'=4] {'dp'}, dimensions={0}, use_global_device_ids=true | all-gather | bytes 995328 | tf_op jit(solution)/shard_map/all_gather | solution.py:126
  340.1 1.2 copy.54
  341.5 25.0 %all-reduce = (f32[192]{0:T(256)}, f32[192]{0:T(256)}, f32[768]{0:T(1024)}, f32[768]{0:T(1024)}, f32[768]{0:T(1024)}, /*index=5*/f32[768]{0:T(1024)}, f32[768]{0:T(1024)}, f32[768]{0:T(1024)}, f32[768]{0:T(1024)}) all-reduce(f32[192]{0:T(256)S(1)} %reduce_sum.296, ...), channel_id=1, replica_groups=mesh['dp'=8,'tensor'=4] {'dp'}, use_global_device_ids=true, to_apply=%region_34.35 | all-reduce | flops 5760 | bytes 46080 | tf_op jit(solution)/shard_map/psum | solution.py:191
  366.4 19.4 %all-reduce.11.cloned.1.call-done = f32[512,768]{1,0:T(8,128)} async-done(((f32[512,768]{1,0:T(8,128)}), f32[512,768]{1,0:T(8,128)}) %all-reduce.11.cloned.1.call-update) | async-done | bytes 1572880 | tf_op jit(solution)/shard_map/psum | solution.py:190
  385.8 2.7 add.267
  388.6 114.3 %all-reduce.13.cloned.1.call-done = (f32[768,192]{0,1:T(8,128)}, f32[768,192]{0,1:T(8,128)}, f32[768,192]{0,1:T(8,128)}, f32[192,768]{1,0:T(8,128)}, f32[768,768]{1,0:T(8,128)}, /*index=5*/f32[768,768]{1,0:T(8,128)}) async-done(((f32[768,192]{0,1:T(8,128)}, f32[768,192]{0,1:T(8,128)}, f32[768,192]{0,1:T(8,128)}, f32[192,768]{1,0:T(8,128)}, f32[768,768]{1,0:T(8,128)}, /*index=5*/f32[768,768]{1,0:T(8,128)}), ...) | async-done | bytes 7077904 | tf_op jit(solution)/shard_map/psum | solution.py:191
  502.9 2.0 copy.76
  505.0 0.8 copy.77
  505.8 0.8 copy.78
  507.4 1.4 copy.80
  508.8 1.1 copy-done.10
  509.9 1.4 copy.81
  (173 shorter events, 16.1 us)
Async XLA Ops:
  7.2 116.2 %copy-start = (bf16[768,768]{1,0:T(8,128)(2,1)S(1)}, bf16[768,768]{1,0:T(8,128)(2,1)}, u32[]{:S(2)}) copy-start(bf16[768,768]{1,0:T(8,128)(2,1)} %param.42) | copy-start | bytes 3538948
  7.2 3.1 copy-start.4
  7.2 3.1 copy-start.27
  7.2 3.1 copy-start.56
  7.2 194.9 %all-reduce.7.cloned.1.call-start = ((), (), s32[]{:S(2)}) async-start(), calls=%async_computation | async-start | bytes 3145728 | tf_op jit(solution)/shard_map/psum | solution.py:111
  8.6 4.6 copy-start.12
  11.6 1.7 copy-start.8
  12.8 1.5 copy-start.41
  14.3 3.6 copy-start.18
  14.7 108.0 %copy-start.50 = (f32[768]{0:T(1024)S(1)}, f32[768]{0:T(1024)}, u32[]{:S(2)}) copy-start(f32[768]{0:T(1024)} %param.39) | copy-start | bytes 9220
  14.7 37.5 %collective-permute-start = (f32[512,768]{1,0:T(8,128)S(1)}, f32[512,768]{1,0:T(8,128)S(1)}, u32[]{:S(2)}, u32[]{:S(2)}) collective-permute-start(f32[512,768]{1,0:T(8,128)S(1)} %fusion.70), channel_id=1, source_target_pairs={{0,1},{1,0},{2,3},{3,2},{4,5},{5,4},{6,7},{7,6},{8,9},{9,8},{10,11... | collective-permute-start | bytes 4718600 | tf_op jit(solution)/shard_map/ppermute | solution.py:20
  52.4 70.2 %collective-permute-start.1 = (f32[512,768]{1,0:T(8,128)S(1)}, f32[512,768]{1,0:T(8,128)S(1)}, u32[]{:S(2)}, u32[]{:S(2)}) collective-permute-start(f32[512,768]{1,0:T(8,128)S(1)} %add.238), channel_id=1, source_target_pairs={{0,2},{1,3},{2,0},{3,1},{4,6},{5,7},{6,4},{7,5},{8,10},{9,11},{10,... | collective-permute-start | bytes 4718600 | tf_op jit(solution)/shard_map/ppermute | solution.py:20
  123.8 6.3 %copy-start.53 = (bf16[768,768]{1,0:T(8,128)(2,1)S(1)}, bf16[768,768]{1,0:T(8,128)(2,1)}, u32[]{:S(2)}) copy-start(bf16[768,768]{1,0:T(8,128)(2,1)} %param.44) | copy-start | bytes 3538948
  132.0 159.9 %all-reduce.9.cloned.1.call-start = ((), (), s32[]{:S(2)}) async-start(), calls=%async_computation.1 | async-start | bytes 3145728 | tf_op jit(solution)/shard_map/psum | solution.py:151
  204.1 2.1 copy-start.5
  204.2 2.0 copy-start.37
  205.1 5.9 %copy-start.39 = (f32[512]{0:T(512)}, f32[512]{0:T(512)S(1)}, u32[]{:S(2)}) copy-start(f32[512]{0:T(512)S(1)} %add_rsqrt_fusion) | copy-start | bytes 6148
  209.0 2.0 copy-start.35
  212.4 4.0 copy-start.6
  212.4 4.0 copy-start.38
  212.4 4.0 copy-start.40
  212.4 4.0 copy-start.44
  212.4 4.0 copy-start.46
  216.4 1.6 copy-start.54
  216.4 2.0 copy-start.61
  216.4 2.6 copy-start.62
  217.9 2.8 copy-start.7
  223.6 162.2 %all-reduce.11.cloned.1.call-start = ((), (), s32[]{:S(2)}) async-start(), calls=%async_computation.2 | async-start | bytes 3145728 | tf_op jit(solution)/shard_map/psum | solution.py:190
  294.7 2.6 copy-start.9
  295.2 3.1 copy-start.2
  295.2 2.0 copy-start.13
  295.2 2.0 copy-start.42
  298.3 2.3 copy-start.21
  307.6 7.0 %copy-start.14 = (bf16[768,192]{0,1:T(8,128)(2,1)S(1)}, bf16[768,192]{0,1:T(8,128)(2,1)}, u32[]{:S(2)}) copy-start(bf16[768,192]{0,1:T(8,128)(2,1)} %param.34) | copy-start | bytes 884740
  317.6 4.0 copy-start.52
  317.6 185.3 %all-reduce.13.cloned.1.call-start = ((), (), s32[]{:S(2)}) async-start(), calls=%async_computation.3 | async-start | bytes 14155776 | tf_op jit(solution)/shard_map/psum | solution.py:191
  317.6 3.9 copy-start.60
  325.1 2.3 copy-start.3
  325.1 2.3 copy-start.19
  328.6 12.9 %copy-start.47 = (f32[768]{0:T(1024)S(1)}, f32[768]{0:T(1024)}, u32[]{:S(2)}) copy-start(f32[768]{0:T(1024)} %get-tuple-element.140) | copy-start | bytes 9220
  328.6 12.9 %copy-start.48 = (f32[768]{0:T(1024)S(1)}, f32[768]{0:T(1024)}, u32[]{:S(2)}) copy-start(f32[768]{0:T(1024)} %get-tuple-element.146) | copy-start | bytes 9220
  328.6 12.9 %copy-start.49 = (f32[768]{0:T(1024)S(1)}, f32[768]{0:T(1024)}, u32[]{:S(2)}) copy-start(f32[768]{0:T(1024)} %get-tuple-element.219) | copy-start | bytes 9220
  502.9 2.1 copy-start.24
  502.9 2.9 copy-start.23
  502.9 3.7 copy-start.22
  504.9 2.5 copy-start.11
  507.4 2.5 copy-start.10
  507.4 3.9 copy-start.1
  (21 other events, 20.2 us)
Sparse Core Ops, SparseCore 0:
  132.1 69.9 all-reduce.6
  223.8 68.1 all-reduce.8
  317.7 68.1 all-reduce.10
  390.9 111.9 all-reduce.12
